TPU v7x, 32 devices: a whole 2x2x4 slice. The times are simulated.
32 devices in a mesh: wide: 8 (over z, x), narrow: 4 (over y, core).
Axes of the slice: x: 2, y: 2, z: 4, core: 2. Of those that a mesh axis runs over, the one named last changes fastest.
Arguments:
- tokens: bfloat16 [24576, 768], P('wide'), may hold values from -6 to 6
- qkv_weight: bfloat16 [3, 768, 768], P(None, None, 'narrow'), may hold values from -0.21875 to 0.21875
- out_weight: bfloat16 [768, 768], P('narrow'), may hold values from -0.875 to 0.875
- norm_bias: float32 [6, 768], replicated, as said below
- up_weight: bfloat16 [2, 768, 3072], P(None, None, 'narrow'), may hold values from -0.21875 to 0.21875
- down_weight: bfloat16 [3072, 768], P('narrow'), may hold values from -0.15625 to 0.15625
- window_lengths: int32 [48], P('wide'), may hold values from 64 to 512, as said below
- cot_out: bfloat16 [24576, 768], P('wide'), may hold values from -6 to 6
Outputs:
- block_out: bfloat16 [24576, 768], P('wide')
- input_grad: float32 [24576, 768], P('wide')
- qkv_grad: float32 [3, 768, 768], P(None, 'wide', 'narrow')
- out_grad: float32 [768, 768], P('narrow', 'wide')
- up_grad: float32 [2, 768, 3072], P(None, 'wide', 'narrow')
- down_grad: float32 [3072, 768], P('narrow', 'wide')
- norm_bias_grad: float32 [6, 768], P(None, 'wide')
Inputs may be any that keep to these rules, and one draw needn't show every extreme that they name: `window_lengths`: keys at or past a window's length are padding; some window holds exactly 512 and some exactly 64. `norm_bias`: rows 0 and 3 lie between 0.5 and 2.
All inputs are finite; a program needn't handle non-finite values.
Results may differ from a plain program's by a relative error of at most 0.025.
Values may be sent and summed in bfloat16 or wider, within the bound.
A program may use at most 192 MiB of HBM per device.

v0:
```python
import math
import jax
import jax.numpy as jnp
from jax import lax
from jax.sharding import PartitionSpec as P

HEADS = 12
HEAD_DIM = 64


def norm_parts(value, gain, shift):
    center = value - jnp.mean(value, axis=-1, keepdims=True)
    spread = jnp.mean(center * center, axis=-1, keepdims=True)
    recip = lax.rsqrt(spread + 1e-05)
    normed = center * recip
    return (normed * gain + shift, normed, recip)


def norm_backward(grad_out, normed, recip, gain):
    scaled = grad_out * gain
    inner = jnp.mean(scaled * normed, axis=-1, keepdims=True)
    grad_in = recip * (scaled - jnp.mean(scaled, axis=-1, keepdims=True) - normed * inner)
    return (grad_in, jnp.sum(grad_out * normed, axis=0), jnp.sum(grad_out, axis=0))


def shards(
    tokens, qkv_weight, out_weight, norm_bias, up_weight, down_weight, window_lengths, cot_out
):
    head_count = qkv_weight.shape[2] // HEAD_DIM
    group_width = qkv_weight.shape[2]
    first_head = lax.axis_index("narrow") * head_count
    slopes = 2.0 ** (-8.0 * (first_head + jnp.arange(head_count) + 1).astype(jnp.float32) / HEADS)
    token_count = tokens.shape[0]
    windows = window_lengths.shape[0]
    window_len = token_count // windows
    score_scale = 1.0 / math.sqrt(HEAD_DIM)
    position = jnp.arange(window_len)
    distance = jnp.abs(position[:, None] - position[None, :]).astype(jnp.float32)

    def score_block(query, key_rows, key_limit):
        raw_scores = jnp.einsum("qhc,khc->hqk", query, key_rows, preferred_element_type=jnp.float32)
        logits = raw_scores * score_scale - slopes[:, None, None] * distance[None]
        return jnp.where(position[None, None, :] < key_limit, logits, -1e30)

    def window_forward(item):
        window_block, key_limit = item
        logits = score_block(window_block[0], window_block[1], key_limit)
        row_top = jnp.max(logits, axis=-1, keepdims=True)
        exponent = jnp.exp(logits - row_top)
        row_total = jnp.sum(exponent, axis=-1, keepdims=True)
        soft_low = (exponent / row_total).astype(jnp.bfloat16)
        log_total = (row_top + jnp.log(row_total))[..., 0]
        result = jnp.einsum(
            "hqk,khc->qhc", soft_low, window_block[2], preferred_element_type=jnp.float32
        )
        return (result.astype(jnp.bfloat16), log_total)

    def window_backward(item):
        window_block, grad_result, log_total, key_limit = item
        logits = score_block(window_block[0], window_block[1], key_limit)
        soft = jnp.exp(logits - log_total[..., None])
        grad_soft = jnp.einsum(
            "qhc,khc->hqk", grad_result, window_block[2], preferred_element_type=jnp.float32
        )
        row_inner = jnp.sum(soft * grad_soft, axis=-1, keepdims=True)
        grad_logit = (soft * (grad_soft - row_inner) * score_scale).astype(jnp.bfloat16)
        grad_query = jnp.einsum(
            "hqk,khc->qhc", grad_logit, window_block[1], preferred_element_type=jnp.float32
        )
        grad_key = jnp.einsum(
            "hqk,qhc->khc", grad_logit, window_block[0], preferred_element_type=jnp.float32
        )
        grad_value = jnp.einsum(
            "hqk,qhc->khc",
            soft.astype(jnp.bfloat16),
            grad_result,
            preferred_element_type=jnp.float32,
        )
        return jnp.stack([grad_query, grad_key, grad_value]).astype(jnp.bfloat16)

    source = tokens.astype(jnp.float32)
    projected = jnp.einsum(
        "td,kdf->ktf", tokens, qkv_weight, preferred_element_type=jnp.float32
    ).astype(jnp.bfloat16)
    window_blocks = jnp.moveaxis(
        projected.reshape(3, windows, window_len, head_count, HEAD_DIM), 1, 0
    )
    attended, log_totals = lax.map(window_forward, (window_blocks, window_lengths))
    attended = attended.reshape(token_count, group_width)
    attn_part = jnp.dot(attended, out_weight, preferred_element_type=jnp.float32)
    attn_branch = lax.psum(attn_part.astype(jnp.bfloat16), "narrow").astype(jnp.float32)
    hidden, normed_one, recip_one = norm_parts(
        attn_branch + norm_bias[2] + source, norm_bias[0], norm_bias[1]
    )
    hidden_low = hidden.astype(jnp.bfloat16)
    gate_up = jnp.einsum("td,kdf->ktf", hidden_low, up_weight, preferred_element_type=jnp.float32)

    def geglu(gate_val, up_val):
        return jax.nn.gelu(gate_val, approximate=False) * up_val

    activation_full, geglu_pull = jax.vjp(geglu, gate_up[0], gate_up[1])
    activation = activation_full.astype(jnp.bfloat16)
    ffn_part = jnp.dot(activation, down_weight, preferred_element_type=jnp.float32)
    ffn_branch = lax.psum(ffn_part.astype(jnp.bfloat16), "narrow").astype(jnp.float32)
    output, normed_two, recip_two = norm_parts(
        ffn_branch + norm_bias[5] + hidden, norm_bias[3], norm_bias[4]
    )
    block_out = output.astype(jnp.bfloat16)
    cotangent = cot_out.astype(jnp.float32)
    grad_second, grad_gain_two, grad_shift_two = norm_backward(
        cotangent, normed_two, recip_two, norm_bias[3]
    )
    grad_down_bias = jnp.sum(grad_second, axis=0)
    grad_second_low = grad_second.astype(jnp.bfloat16)
    down_grad = jnp.einsum(
        "tf,td->fd", activation, grad_second_low, preferred_element_type=jnp.float32
    )
    grad_activation = jnp.einsum(
        "td,fd->tf", grad_second_low, down_weight, preferred_element_type=jnp.float32
    )
    grad_gate, grad_up_val = geglu_pull(grad_activation)
    grad_gate_up = jnp.stack([grad_gate, grad_up_val]).astype(jnp.bfloat16)
    up_grad = jnp.einsum(
        "td,ktf->kdf", hidden_low, grad_gate_up, preferred_element_type=jnp.float32
    )
    hidden_part = jnp.einsum(
        "ktf,kdf->td", grad_gate_up, up_weight, preferred_element_type=jnp.float32
    )
    small_ffn = jnp.stack([grad_gain_two, grad_shift_two, grad_down_bias])
    grad_hidden = grad_second + lax.psum(hidden_part.astype(jnp.bfloat16), "narrow").astype(
        jnp.float32
    )
    grad_first, grad_gain_one, grad_shift_one = norm_backward(
        grad_hidden, normed_one, recip_one, norm_bias[0]
    )
    grad_out_bias = jnp.sum(grad_first, axis=0)
    grad_first_low = grad_first.astype(jnp.bfloat16)
    out_grad = jnp.einsum("tf,td->fd", attended, grad_first_low, preferred_element_type=jnp.float32)
    grad_attended = jnp.einsum(
        "td,fd->tf", grad_first_low, out_weight, preferred_element_type=jnp.float32
    )
    grad_attended = grad_attended.astype(jnp.bfloat16).reshape(
        windows, window_len, head_count, HEAD_DIM
    )
    grad_blocks = lax.map(
        window_backward, (window_blocks, grad_attended, log_totals, window_lengths)
    )
    grad_projected = jnp.moveaxis(grad_blocks, 1, 0).reshape(3, token_count, group_width)
    qkv_grad = jnp.einsum("td,ktf->kdf", tokens, grad_projected, preferred_element_type=jnp.float32)
    source_part = jnp.einsum(
        "ktf,kdf->td", grad_projected, qkv_weight, preferred_element_type=jnp.float32
    )
    small_attn = jnp.stack([grad_gain_one, grad_shift_one, grad_out_bias])
    input_grad = grad_first + lax.psum(source_part.astype(jnp.bfloat16), "narrow").astype(
        jnp.float32
    )
    small_all = jnp.concatenate([small_attn, small_ffn], axis=0)
    qkv_share, out_share, up_share, down_share, small_share = (
        lax.psum_scatter(qkv_grad, "wide", scatter_dimension=1, tiled=True),
        lax.psum_scatter(out_grad, "wide", scatter_dimension=1, tiled=True),
        lax.psum_scatter(up_grad, "wide", scatter_dimension=1, tiled=True),
        lax.psum_scatter(down_grad, "wide", scatter_dimension=1, tiled=True),
        lax.psum_scatter(small_all, "wide", scatter_dimension=1, tiled=True),
    )
    return (block_out, input_grad, qkv_share, out_share, up_share, down_share, small_share)


def solution(mesh):
    placed = (
        P("wide", None),
        P(None, None, "narrow"),
        P("narrow", None),
        P(),
        P(None, None, "narrow"),
        P("narrow", None),
        P("wide"),
        P("wide", None),
    )
    return jax.shard_map(
        shards,
        mesh=mesh,
        in_specs=placed,
        out_specs=(
            P("wide", None),
            P("wide", None),
            P(None, "wide", "narrow"),
            P("narrow", "wide"),
            P(None, "wide", "narrow"),
            P("narrow", "wide"),
            P(None, "wide"),
        ),
        check_vma=False,
    )
```

profile of v0, /device:TPU:0, one launch (start us, length us, event | category | flops | bytes accessed | tf_op | source)
XLA Modules:
  0.0 1051.4 jit_solution(7509393685170289483)
XLA Ops:
  7.2 7.5 fusion.106
  14.7 8.1 reshape.169
  28.1 56.5 %while.24 = (s32[]{:T(128)}, bf16[6,512,3,64]{1,3,2,0:T(8,128)(2,1)}, f32[6,3,512]{2,1,0:T(4,128)}, bf16[6,3,512,3,64]{2,4,3,1,0:T(8,128)(2,1)}, s32[6]{0:T(128)...) while((s32[]{:T(128)}, bf16[6,512,3,64]{1,3,2,0:T(8,128)(2,1)}, ...), condition=%wide.region_3.4_spmd.clone, body=%wide.region_0.3_spmd.clone.sunk | while | flops 210074640 | bytes 24958668 | solution.py:88
  93.0 96.5 %all-reduce.7.cloned.1.call-done = bf16[3072,768]{1,0:T(8,128)(2,1)} async-done(((bf16[3072,768]{1,0:T(8,128)(2,1)}), bf16[3072,768]{1,0:T(8,128)(2,1)}) %all-reduce.7.cloned.1.call-update) | async-done | bytes 4718608 | tf_op jit(solution)/shard_map/psum | solution.py:91
  199.4 11.3 %convolution_bitcast_fusion = f32[2,3072,768]{2,1,0:T(8,128)} fusion(bf16[2,768,768]{2,1,0:T(8,128)(2,1)S(1)} %copy-done, f32[768]{0:T(1024)S(1)} %get-tuple-element.201, f32[768]{0:T(1024)S(1)} %get-tuple-element.202, bf16[3072,768]{1,0:T(8,128)(2,1)S(1)} %bitcast.244, bf16[3072,768]{1,0:T(8,128)(2,1)S(1)} %copy-done.2, f32[3072]{0:T(1024)S(1)} %add_rsqrt_fusion.1, ...), kind=kOutput, calls=%fused_computation.122 | convolution fusion | flops 7268990976 | bytes 30704640 | tf_op jit(solution)/shard_map/td,kdf->ktf/dot_general | solution.py:96
  210.7 22.9 %multiply_convert_fusion.2 = (bf16[3072,768]{1,0:T(8,128)(2,1)S(1)}, f32[3072,768]{1,0:T(8,128)}) fusion(f32[2,3072,768]{2,1,0:T(8,128)} %convolution_bitcast_fusion), kind=kLoop, calls=%fused_computation.100 | loop fusion | flops 155713536 | bytes 33030144 | tf_op jit(solution)/shard_map/convert_element_type | solution.py:102
  241.7 93.8 %all-reduce.9.cloned.1.call-done = bf16[3072,768]{1,0:T(8,128)(2,1)} async-done(((bf16[3072,768]{1,0:T(8,128)(2,1)}), bf16[3072,768]{1,0:T(8,128)(2,1)}) %all-reduce.9.cloned.1.call-update) | async-done | bytes 4718608 | tf_op jit(solution)/shard_map/psum | solution.py:104
  335.5 7.6 fusion.129
  356.8 19.1 %fusion.102 = (bf16[1,3072,768]{2,1,0:T(8,128)(2,1)}, bf16[1,3072,768]{2,1,0:T(8,128)(2,1)}) fusion(f32[3072,768]{1,0:T(8,128)} %get-tuple-element.236, f32[2,3072,768]{2,1,0:T(8,128)} %convolution_bitcast_fusion, bf16[768,768]{1,0:T(8,128)(2,1)} %param.17, f32[3072,768]{1,0:T(8,128)} %get-tuple-element.241), kind=kOutput, calls=%fused_computation.134 | convolution fusion | flops 3668705280 | bytes 48365568 | tf_op jit(solution)/shard_map/td,fd->tf/dot_general | solution.py:118
  376.0 11.6 %bitcast_convert_fusion.1 = bf16[3072,768]{1,0:T(8,128)(2,1)} fusion(bf16[2,768,768]{2,1,0:T(8,128)(2,1)S(1)} %copy-done, bf16[1,3072,768]{2,1,0:T(8,128)(2,1)} %get-tuple-element.240, bf16[1,3072,768]{2,1,0:T(8,128)(2,1)} %get-tuple-element.239), kind=kOutput, calls=%fused_computation.77 | convolution fusion | flops 7254835200 | bytes 16515072 | tf_op jit(solution)/shard_map/ktf,kdf->td/dot_general | solution.py:126
  387.8 94.1 %all-reduce.11.cloned.1.call-done = bf16[3072,768]{1,0:T(8,128)(2,1)} async-done(((bf16[3072,768]{1,0:T(8,128)(2,1)}), bf16[3072,768]{1,0:T(8,128)(2,1)}) %all-reduce.11.cloned.1.call-update) | async-done | bytes 4718608 | tf_op jit(solution)/shard_map/psum | solution.py:130
  481.9 11.2 %multiply_reduce_fusion.1 = (f32[768]{0:T(1024)S(1)}, f32[3072]{0:T(1024)S(1)}, f32[3072]{0:T(1024)S(1)}, f32[768]{0:T(1024)S(1)}, f32[768]{0:T(1024)S(1)}) fusion(f32[3072,768]{1,0:T(8,128)} %get-tuple-element.241, bf16[3072,768]{1,0:T(8,128)(2,1)} %all-reduce.11.cloned.1.call-done, f32[3072]{0:T(1024)S(1)} %add_rsqrt_fusion.1, ...), kind=kLoop, calls=%fused_computation.91 | loop fusion | flops 37740288 | bytes 23657472 | tf_op jit(solution)/shard_map/reduce_sum | solution.py:23
  493.2 12.8 %fusion.128 = (f32[768]{0:T(1024)S(1)}, f32[3072,768]{1,0:T(8,128)}) fusion(f32[3072]{0:T(1024)S(1)} %broadcast_multiply_fusion, f32[3072]{0:T(1024)S(1)} %broadcast_multiply_fusion.5, bf16[3072,768]{1,0:T(8,128)(2,1)} %param.12, f32[768]{0:T(1024)S(1)} %get-tuple-element.203, bf16[3072,768]{1,0:T(8,128)(2,1)} %all-reduce.7.cloned.1.call-done, ...), kind=kLoop, calls=%fused_computation.166 | loop fusion | flops 33029376 | bytes 33088512 | tf_op jit(solution)/shard_map/reduce_sum | solution.py:136
  513.7 17.7 %fusion.116 = f32[2,768,768]{1,2,0:T(8,128)} fusion(bf16[1,3072,768]{2,1,0:T(8,128)(2,1)} %get-tuple-element.240, bf16[1,3072,768]{2,1,0:T(8,128)(2,1)} %get-tuple-element.239, f32[768]{0:T(1024)S(1)} %get-tuple-element.201, f32[768]{0:T(1024)S(1)} %get-tuple-element.202, bf16[3072,768]{1,0:T(8,128)(2,1)} %param.12, ...), kind=kOutput, calls=%fused_computation.145 | convolution fusion | flops 7273709568 | bytes 23626752 | tf_op jit(solution)/shard_map/td,ktf->kdf/dot_general | solution.py:123
  531.4 8.2 copy.46
  549.5 143.8 %while.25 = (s32[]{:T(128)}, bf16[6,3,512,3,64]{2,4,3,1,0:T(8,128)(2,1)}, bf16[6,3,512,3,64]{2,4,3,1,0:T(8,128)(2,1)}, s32[6]{0:T(128)S(1)}, f32[6,3,512]{2,1,0:...) while((s32[]{:T(128)}, ...), condition=%wide.region_17.18_spmd.clone, body=%wide.region_15.17_spmd.clone.sunk | while | flops 518754816 | bytes 39869124 | solution.py:145
  699.9 8.2 reshape.172
  708.1 7.7 bitcast_convert_fusion
  730.1 10.4 fusion.112
  745.0 61.0 %all-reduce.15.cloned.1.call-done = f32[2,768,768]{2,0,1:T(2,128)} async-done(((f32[2,768,768]{2,0,1:T(2,128)}), f32[2,768,768]{2,0,1:T(2,128)}) %all-reduce.15.cloned.1.call-update) | async-done | bytes 4718608
  807.9 93.6 %all-reduce.13.cloned.1.call-done = bf16[3072,768]{1,0:T(8,128)(2,1)} async-done(((bf16[3072,768]{1,0:T(8,128)(2,1)}), bf16[3072,768]{1,0:T(8,128)(2,1)}) %all-reduce.13.cloned.1.call-update) | async-done | bytes 4718608 | tf_op jit(solution)/shard_map/psum | solution.py:154
  901.5 9.7 convert_add_fusion
  911.1 61.2 %reduce-scatter.13.cloned.1.call-done = f32[96,576]{1,0:T(8,128)} async-done(((f32[768,576]{1,0:T(8,128)}), f32[96,576]{1,0:T(8,128)}) %reduce-scatter.13.cloned.1.call-update) | async-done | bytes 221200
  974.2 70.2 %reduce-scatter.11.cloned.1.call-done = f32[768,96]{0,1:T(8,128)} async-done(((f32[768,768]{0,1:T(8,128)}), f32[768,96]{0,1:T(8,128)}) %reduce-scatter.11.cloned.1.call-update) | async-done | bytes 294928 | tf_op jit(solution)/shard_map/reduce_scatter | solution.py:162
  (228 shorter events, 291.3 us)
Async XLA Ops:
  7.2 192.2 %copy-start = (bf16[2,768,768]{2,1,0:T(8,128)(2,1)S(1)}, bf16[2,768,768]{2,1,0:T(8,128)(2,1)}, u32[]{:S(2)}) copy-start(bf16[2,768,768]{2,1,0:T(8,128)(2,1)} %param.16) | copy-start | bytes 7077892
  7.2 182.4 %all-reduce.7.cloned.1.call-start = ((), (), s32[]{:S(2)}) async-start(), calls=%async_computation.4 | async-start | bytes 9437184 | tf_op jit(solution)/shard_map/psum | solution.py:91
  14.7 13.4 %copy-start.12 = (s32[6]{0:T(128)S(1)}, s32[6]{0:T(128)}, u32[]{:S(2)}) copy-start(s32[6]{0:T(128)} %param.18) | copy-start | bytes 76
  86.6 6.4 copy-start.9
  92.7 102.4 %slice-start = ((s8[4718592]{0:T(1024)(128)(4,1)}), s8[524288]{0:T(1024)(128)(4,1)S(1)}, s32[]{:S(2)}) async-start(s8[4718592]{0:T(1024)(128)(4,1)} %bitcast.243), calls=%async_computation.13 | async-start | bytes 1048576
  92.7 242.8 %all-reduce.9.cloned.1.call-start = ((), (), s32[]{:S(2)}) async-start(), calls=%async_computation.5 | async-start | bytes 9437184 | tf_op jit(solution)/shard_map/psum | solution.py:104
  189.6 5.5 copy-start.2
  189.6 6.4 slice-start.1
  210.6 25.0 %copy-start.10 = (bf16[768,768]{1,0:T(8,128)(2,1)S(1)}, bf16[768,768]{1,0:T(8,128)(2,1)}, u32[]{:S(2)}) copy-start(bf16[768,768]{1,0:T(8,128)(2,1)} %param.17) | copy-start | bytes 3538948
  241.1 240.8 %all-reduce.11.cloned.1.call-start = ((), (), s32[]{:S(2)}) async-start(), calls=%async_computation.6 | async-start | bytes 9437184 | tf_op jit(solution)/shard_map/psum | solution.py:130
  343.1 2.3 slice-start.3
  387.6 354.3 %reduce-scatter.17.cloned.1.call-start = ((), (), s32[]{:S(2)}) async-start(), calls=%async_computation.11 | async-start | bytes 442368
  481.9 11.3 %copy-start.4 = (bf16[3072,768]{1,0:T(8,128)(2,1)S(1)}, bf16[3072,768]{1,0:T(8,128)(2,1)}, u32[]{:S(2)}) copy-start(bf16[3072,768]{1,0:T(8,128)(2,1)} %all-reduce.11.cloned.1.call-done) | copy-start | bytes 14155780
  493.2 13.9 %copy-start.6 = (bf16[24,8,6,512]{3,1,2,0:T(8,128)(2,1)S(1)}, bf16[24,8,6,512]{3,1,2,0:T(8,128)(2,1)}, u32[]{:S(2)}) copy-start(bf16[24,8,6,512]{3,1,2,0:T(8,128)(2,1)} %copy-done.5) | copy-start | bytes 3538948
  507.0 236.3 %reduce-scatter.15.cloned.1.call-start = ((), (), s32[]{:S(2)}) async-start(), calls=%async_computation.10 | async-start | bytes 884736
  513.6 292.3 %all-reduce.15.cloned.1.call-start = ((), (), s32[]{:S(2)}) async-start(), calls=%async_computation.12 | async-start | bytes 9437184
  531.4 8.5 copy-start.8
  539.7 9.8 copy-start.13
  539.7 361.8 %all-reduce.13.cloned.1.call-start = ((), (), s32[]{:S(2)}) async-start(), calls=%async_computation.7 | async-start | bytes 9437184 | tf_op jit(solution)/shard_map/psum | solution.py:154
  693.3 14.9 %copy-start.11 = (bf16[3,768,192]{1,2,0:T(8,128)(2,1)S(1)}, bf16[3,768,192]{1,2,0:T(8,128)(2,1)}, u32[]{:S(2)}) copy-start(bf16[3,768,192]{1,2,0:T(8,128)(2,1)} %param.13) | copy-start | bytes 2654212
  715.9 256.4 %reduce-scatter.13.cloned.1.call-start = ((), (), s32[]{:S(2)}) async-start(), calls=%async_computation.9 | async-start | bytes 2211840
  730.1 10.5 %copy-start.14 = (u32[32]{0:T(128)S(1)}, u32[32]{0:T(128)}, u32[]{:S(2)}) copy-start(u32[32]{0:T(128)} %constant.135) | copy-start | bytes 388
  730.1 314.3 %reduce-scatter.11.cloned.1.call-start = ((), (), s32[]{:S(2)}) async-start(), calls=%async_computation.8 | async-start | bytes 2654208 | tf_op jit(solution)/shard_map/reduce_scatter | solution.py:162
  807.1 237.3 %copy-start.1 = (bf16[2,768,768]{2,1,0:T(8,128)(2,1)S(1)}, bf16[2,768,768]{2,1,0:T(8,128)(2,1)}, u32[]{:S(2)}) copy-start(bf16[2,768,768]{2,1,0:T(8,128)(2,1)} %param.16) | copy-start | bytes 7077892
  (9 other events, 15.4 us)
Sparse Core Ops, SparseCore 0:
  92.8 96.7 all-reduce.6
  241.3 94.1 all-reduce.8
  387.7 94.1 all-reduce.10
  507.1 61.5 reduce-scatter.16
  571.9 61.4 reduce-scatter.14
  637.3 168.6 all-reduce.14
  808.4 93.0 all-reduce.12
  905.4 66.9 reduce-scatter.12
  976.4 67.9 reduce-scatter.10
where the time goes:
time: 1060 us; the launch traced here: 1050 us
  waiting for transfers between devices  570 us (54%)
  matrix products  271 us (26%)
  other arithmetic  108 us (10%)
  local copies, waits for them, and re-layouts  84.4 us (8%)
  between operations  15.3 us (1%)
    unnamed x13, waiting for transfers between devices  122 us
    psum x1, waiting for transfers between devices, shards(): lax.psum(attn_part.astype(jnp.bfloat16), 'narrow').astype(jnp.float32)  96.5 us
    psum x1, waiting for transfers between devices, shards(): lax.psum(hidden_part.astype(jnp.bfloat16), 'narrow').astype(jnp.float32)  94.1 us
    psum x1, waiting for transfers between devices, shards(): lax.psum(ffn_part.astype(jnp.bfloat16), 'narrow').astype(jnp.float32)  93.8 us
    psum x1, waiting for transfers between devices, shards(): lax.psum(source_part.astype(jnp.bfloat16), 'narrow').astype(jnp.float32)  93.6 us
    reduce_scatter x1, waiting for transfers between devices, shards(): lax.psum_scatter(down_grad, 'wide', scatter_dimension=1, tiled=True)  70.2 us
    dot_general x6, matrix products, window_backward(): jnp.einsum('hqk,khc->qhc', grad_logit, window_block[1], preferred_element...  34.7 us
    dot_general x6, matrix products, window_backward(): jnp.einsum('hqk,qhc->khc', grad_logit, window_block[0], preferred_element...  34.3 us
  transfers between devices with their start and end apart: 9, of which 7 were waited for; matrix products, arithmetic and copies ran while one was open for 24% of the time, Pallas kernels for 0%

commit v1 on v0

--- a/solution.py
+++ b/solution.py
@@ -88,7 +88,13 @@
     attended, log_totals = lax.map(window_forward, (window_blocks, window_lengths))
     attended = attended.reshape(token_count, group_width)
     attn_part = jnp.dot(attended, out_weight, preferred_element_type=jnp.float32)
-    attn_branch = lax.psum(attn_part.astype(jnp.bfloat16), "narrow").astype(jnp.float32)
+
+    def step_on_panel(tile_in):
+        before = lax.all_gather(tile_in, "narrow")
+        found_now = jnp.sum(before, 0)
+        return found_now
+
+    attn_branch = step_on_panel(attn_part.astype(jnp.bfloat16)).astype(jnp.float32)
     hidden, normed_one, recip_one = norm_parts(
         attn_branch + norm_bias[2] + source, norm_bias[0], norm_bias[1]
     )

time: 1060 us -> 1100 us (1.038)
  waiting for transfers between devices: 570 us -> 593 us
  other arithmetic: 108 us -> 124 us
    all_gather x0 -> x1, waiting for transfers between devices: none -> 121 us  [step_on_panel(): before = lax.all_gather(tile_in, 'narrow')]
    psum x1 -> x0, waiting for transfers between devices: 96.5 us -> none  [shards(): lax.psum(attn_part.astype(jnp.bfloat16), 'narrow').astype(jnp.float32)]
    reduce_sum x0 -> x1, other arithmetic: none -> 13.5 us  [step_on_panel(): found_now = jnp.sum(before, 0)]
    unnamed x49 -> x61, local copies, waits for them, and re-layouts: 27.6 us -> 25.8 us
  transfers between devices with their start and end apart: 9 -> 9, of which waited for: 7 -> 7; matrix products, arithmetic and copies ran while one was open for 24% -> 23% of each run, Pallas kernels for 0% -> 0%
where the time goes in v1:
time: 1100 us; the launch traced here: 1090 us
  waiting for transfers between devices  593 us (54%)
  matrix products  271 us (25%)
  other arithmetic  124 us (11%)
  local copies, waits for them, and re-layouts  85.5 us (8%)
  between operations  15.4 us (1%)
    unnamed x13, waiting for transfers between devices  122 us
    all_gather x1, waiting for transfers between devices, step_on_panel(): before = lax.all_gather(tile_in, 'narrow')  121 us
    psum x1, waiting for transfers between devices, shards(): lax.psum(ffn_part.astype(jnp.bfloat16), 'narrow').astype(jnp.float32)  93.7 us
    psum x1, waiting for transfers between devices, shards(): lax.psum(source_part.astype(jnp.bfloat16), 'narrow').astype(jnp.float32)  93.6 us
    psum x1, waiting for transfers between devices, shards(): lax.psum(hidden_part.astype(jnp.bfloat16), 'narrow').astype(jnp.float32)  92.7 us
    reduce_scatter x1, waiting for transfers between devices, shards(): lax.psum_scatter(down_grad, 'wide', scatter_dimension=1, tiled=True)  70.2 us
    dot_general x6, matrix products, window_backward(): jnp.einsum('hqk,khc->qhc', grad_logit, window_block[1], preferred_element...  34.7 us
    dot_general x6, matrix products, window_backward(): jnp.einsum('hqk,qhc->khc', grad_logit, window_block[0], preferred_element...  34.3 us
  transfers between devices with their start and end apart: 9, of which 7 were waited for; matrix products, arithmetic and copies ran while one was open for 23% of the time, Pallas kernels for 0%

profile of v1, /device:TPU:0, one launch (start us, length us, event | category | flops | bytes accessed | tf_op | source)
XLA Modules:
  0.0 1092.0 jit_solution(4378262494577133079)
XLA Ops:
  14.7 8.1 reshape.169
  28.1 56.5 %while.24 = (s32[]{:T(128)}, bf16[6,512,3,64]{1,3,2,0:T(8,128)(2,1)}, f32[6,3,512]{2,1,0:T(4,128)}, bf16[6,3,512,3,64]{2,4,3,1,0:T(8,128)(2,1)}, s32[6]{0:T(128)...) while((s32[]{:T(128)}, bf16[6,512,3,64]{1,3,2,0:T(8,128)(2,1)}, ...), condition=%wide.region_3.4_spmd.clone, body=%wide.region_0.3_spmd.clone.sunk | while | flops 210074640 | bytes 24958668 | solution.py:88
  93.5 121.0 %all-gather.3.cloned.1.call-done = bf16[12288,768]{1,0:T(8,128)(2,1)} async-done(((bf16[3072,768]{1,0:T(8,128)(2,1)}), bf16[12288,768]{1,0:T(8,128)(2,1)}) %all-gather.3.cloned.1.call-update) | async-done | bytes 18874384 | tf_op jit(solution)/shard_map/all_gather | solution.py:93
  214.5 13.5 %reduce_sum.156 = bf16[3072,768]{1,0:T(8,128)(2,1)} reduce(bf16[4,3072,768]{2,1,0:T(8,128)(2,1)} %bitcast.248, bf16[]{:T(256)} %constant.66.clone.1), dimensions={0}, to_apply=%region_4.5 | reduce | flops 7077888 | bytes 23592962 | tf_op jit(solution)/shard_map/reduce_sum | solution.py:94
  238.8 11.4 %convolution_bitcast_fusion = f32[2,3072,768]{2,1,0:T(8,128)} fusion(bf16[2,768,768]{2,1,0:T(8,128)(2,1)S(1)} %copy-done, f32[768]{0:T(1024)S(1)} %copy-done.12, f32[768]{0:T(1024)S(1)} %copy-done.8, bf16[3072,768]{1,0:T(8,128)(2,1)S(1)} %bitcast.247, bf16[3072,768]{1,0:T(8,128)(2,1)S(1)} %bitcast.245, f32[3072]{0:T(1024)S(1)} %add_rsqrt_fusion.1, ...), kind=kOutput, calls=%fused_computation.122 | convolution fusion | flops 7268990976 | bytes 30704640 | tf_op jit(solution)/shard_map/td,kdf->ktf/dot_general | solution.py:102
  250.2 22.9 %multiply_convert_fusion.2 = (bf16[3072,768]{1,0:T(8,128)(2,1)S(1)}, f32[3072,768]{1,0:T(8,128)}) fusion(f32[2,3072,768]{2,1,0:T(8,128)} %convolution_bitcast_fusion), kind=kLoop, calls=%fused_computation.100 | loop fusion | flops 155713536 | bytes 33030144 | tf_op jit(solution)/shard_map/convert_element_type | solution.py:108
  281.3 93.7 %all-reduce.6.cloned.1.call-done = bf16[3072,768]{1,0:T(8,128)(2,1)} async-done(((bf16[3072,768]{1,0:T(8,128)(2,1)}), bf16[3072,768]{1,0:T(8,128)(2,1)}) %all-reduce.6.cloned.1.call-update) | async-done | bytes 4718608 | tf_op jit(solution)/shard_map/psum | solution.py:110
  374.9 7.8 fusion.129
  397.1 19.1 %fusion.102 = (bf16[1,3072,768]{2,1,0:T(8,128)(2,1)}, bf16[1,3072,768]{2,1,0:T(8,128)(2,1)}) fusion(f32[3072,768]{1,0:T(8,128)} %get-tuple-element.236, f32[2,3072,768]{2,1,0:T(8,128)} %convolution_bitcast_fusion, bf16[768,768]{1,0:T(8,128)(2,1)} %param.17, f32[3072,768]{1,0:T(8,128)} %get-tuple-element.241), kind=kOutput, calls=%fused_computation.134 | convolution fusion | flops 3668705280 | bytes 48365568 | tf_op jit(solution)/shard_map/td,fd->tf/dot_general | solution.py:124
  416.3 11.6 %bitcast_convert_fusion.1 = bf16[3072,768]{1,0:T(8,128)(2,1)} fusion(bf16[2,768,768]{2,1,0:T(8,128)(2,1)S(1)} %copy-done, bf16[1,3072,768]{2,1,0:T(8,128)(2,1)} %get-tuple-element.240, bf16[1,3072,768]{2,1,0:T(8,128)(2,1)} %get-tuple-element.239), kind=kOutput, calls=%fused_computation.77 | convolution fusion | flops 7254835200 | bytes 16515072 | tf_op jit(solution)/shard_map/ktf,kdf->td/dot_general | solution.py:132
  429.5 92.7 %all-reduce.8.cloned.1.call-done = bf16[3072,768]{1,0:T(8,128)(2,1)} async-done(((bf16[3072,768]{1,0:T(8,128)(2,1)}), bf16[3072,768]{1,0:T(8,128)(2,1)}) %all-reduce.8.cloned.1.call-update) | async-done | bytes 4718608 | tf_op jit(solution)/shard_map/psum | solution.py:136
  522.2 11.7 %multiply_reduce_fusion.1 = (f32[768]{0:T(1024)S(1)}, f32[3072]{0:T(1024)S(1)}, f32[3072]{0:T(1024)S(1)}, f32[768]{0:T(1024)S(1)}, f32[768]{0:T(1024)S(1)}) fusion(f32[3072,768]{1,0:T(8,128)} %get-tuple-element.241, bf16[3072,768]{1,0:T(8,128)(2,1)} %all-reduce.8.cloned.1.call-done, f32[3072]{0:T(1024)} %copy-done.6, f32[3072]{0:T(1024)S(1)} %broadcast_multiply_fusion.5, ...), kind=kLoop, calls=%fused_computation.91 | loop fusion | flops 37740288 | bytes 23657472 | tf_op jit(solution)/shard_map/reduce_sum | solution.py:23
  534.0 12.7 %fusion.128 = (f32[768]{0:T(1024)S(1)}, f32[3072,768]{1,0:T(8,128)}) fusion(f32[3072]{0:T(1024)S(1)} %broadcast_multiply_fusion, f32[3072]{0:T(1024)S(1)} %broadcast_multiply_fusion.5, bf16[3072,768]{1,0:T(8,128)(2,1)} %param.12, f32[768]{0:T(1024)S(1)} %get-tuple-element.203, bf16[3072,768]{1,0:T(8,128)(2,1)} %reduce_sum.156, ...), kind=kLoop, calls=%fused_computation.166 | loop fusion | flops 33029376 | bytes 33088512 | tf_op jit(solution)/shard_map/reduce_sum | solution.py:142
  554.4 17.7 %fusion.116 = f32[2,768,768]{1,2,0:T(8,128)} fusion(bf16[1,3072,768]{2,1,0:T(8,128)(2,1)} %get-tuple-element.240, bf16[1,3072,768]{2,1,0:T(8,128)(2,1)} %get-tuple-element.239, f32[768]{0:T(1024)S(1)} %copy-done.13, f32[768]{0:T(1024)S(1)} %copy-done.9, bf16[3072,768]{1,0:T(8,128)(2,1)} %param.12, bf16[3072,768]{1,0:T(8,128)(2,1)} %reduce_sum.156, ...), kind=kOutput, calls=%fused_computation.145 | convolution fusion | flops 7273709568 | bytes 23626752 | tf_op jit(solution)/shard_map/td,ktf->kdf/dot_general | solution.py:129
  572.1 8.2 copy.46
  590.1 143.8 %while.25 = (s32[]{:T(128)}, bf16[6,3,512,3,64]{2,4,3,1,0:T(8,128)(2,1)}, bf16[6,3,512,3,64]{2,4,3,1,0:T(8,128)(2,1)}, s32[6]{0:T(128)S(1)}, f32[6,3,512]{2,1,0:...) while((s32[]{:T(128)}, ...), condition=%wide.region_17.18_spmd.clone, body=%wide.region_15.17_spmd.clone.sunk | while | flops 518754816 | bytes 39869124 | solution.py:151
  740.6 8.2 reshape.172
  748.8 7.7 bitcast_convert_fusion
  770.8 10.4 fusion.112
  785.6 61.0 %all-reduce.12.cloned.1.call-done = f32[2,768,768]{2,0,1:T(2,128)} async-done(((f32[2,768,768]{2,0,1:T(2,128)}), f32[2,768,768]{2,0,1:T(2,128)}) %all-reduce.12.cloned.1.call-update) | async-done | bytes 4718608
  848.6 93.6 %all-reduce.10.cloned.1.call-done = bf16[3072,768]{1,0:T(8,128)(2,1)} async-done(((bf16[3072,768]{1,0:T(8,128)(2,1)}), bf16[3072,768]{1,0:T(8,128)(2,1)}) %all-reduce.10.cloned.1.call-update) | async-done | bytes 4718608 | tf_op jit(solution)/shard_map/psum | solution.py:160
  942.1 9.7 convert_add_fusion
  951.8 61.2 %reduce-scatter.13.cloned.1.call-done = f32[96,576]{1,0:T(8,128)} async-done(((f32[768,576]{1,0:T(8,128)}), f32[96,576]{1,0:T(8,128)}) %reduce-scatter.13.cloned.1.call-update) | async-done | bytes 221200
  1014.9 70.2 %reduce-scatter.11.cloned.1.call-done = f32[768,96]{0,1:T(8,128)} async-done(((f32[768,768]{0,1:T(8,128)}), f32[768,96]{0,1:T(8,128)}) %reduce-scatter.11.cloned.1.call-update) | async-done | bytes 294928 | tf_op jit(solution)/shard_map/reduce_scatter | solution.py:168
  (242 shorter events, 302.2 us)
Async XLA Ops:
  7.2 231.6 %copy-start = (bf16[2,768,768]{2,1,0:T(8,128)(2,1)S(1)}, bf16[2,768,768]{2,1,0:T(8,128)(2,1)}, u32[]{:S(2)}) copy-start(bf16[2,768,768]{2,1,0:T(8,128)(2,1)} %param.16) | copy-start | bytes 7077892
  7.2 207.3 %all-gather.3.cloned.1.call-start = ((), (), s32[]{:S(2)}) async-start(), calls=%async_computation.8 | async-start | bytes 23592960 | tf_op jit(solution)/shard_map/all_gather | solution.py:93
  14.7 13.4 %copy-start.16 = (s32[6]{0:T(128)S(1)}, s32[6]{0:T(128)}, u32[]{:S(2)}) copy-start(s32[6]{0:T(128)} %param.18) | copy-start | bytes 76
  91.7 283.3 %all-reduce.6.cloned.1.call-start = ((), (), s32[]{:S(2)}) async-start(), calls=%async_computation.4 | async-start | bytes 9437184 | tf_op jit(solution)/shard_map/psum | solution.py:110
  228.1 10.7 slice-start.2
  228.1 10.7 copy-start.8
  228.1 10.7 copy-start.12
  238.8 11.5 %copy-start.6 = (f32[3072]{0:T(1024)}, f32[3072]{0:T(1024)S(1)}, u32[]{:S(2)}) copy-start(f32[3072]{0:T(1024)S(1)} %add_rsqrt_fusion.1) | copy-start | bytes 36868
  250.2 25.0 %copy-start.14 = (bf16[768,768]{1,0:T(8,128)(2,1)S(1)}, bf16[768,768]{1,0:T(8,128)(2,1)}, u32[]{:S(2)}) copy-start(bf16[768,768]{1,0:T(8,128)(2,1)} %param.17) | copy-start | bytes 3538948
  280.7 241.5 %all-reduce.8.cloned.1.call-start = ((), (), s32[]{:S(2)}) async-start(), calls=%async_computation.5 | async-start | bytes 9437184 | tf_op jit(solution)/shard_map/psum | solution.py:136
  427.9 354.6 %reduce-scatter.17.cloned.1.call-start = ((), (), s32[]{:S(2)}) async-start(), calls=%async_computation.11 | async-start | bytes 442368
  429.5 104.4 %copy-start.7 = (f32[3072]{0:T(1024)S(1)}, f32[3072]{0:T(1024)}, u32[]{:S(2)}) copy-start(f32[3072]{0:T(1024)} %copy-done.6) | copy-start | bytes 36868
  429.5 104.4 %copy-start.9 = (f32[768]{0:T(1024)S(1)}, f32[768]{0:T(1024)}, u32[]{:S(2)}) copy-start(f32[768]{0:T(1024)} %get-tuple-element.202) | copy-start | bytes 9220
  522.2 11.7 %copy-start.3 = (bf16[3072,768]{1,0:T(8,128)(2,1)S(1)}, bf16[3072,768]{1,0:T(8,128)(2,1)}, u32[]{:S(2)}) copy-start(bf16[3072,768]{1,0:T(8,128)(2,1)} %all-reduce.8.cloned.1.call-done) | copy-start | bytes 14155780
  547.7 236.3 %reduce-scatter.15.cloned.1.call-start = ((), (), s32[]{:S(2)}) async-start(), calls=%async_computation.10 | async-start | bytes 884736
  554.3 292.3 %all-reduce.12.cloned.1.call-start = ((), (), s32[]{:S(2)}) async-start(), calls=%async_computation.12 | async-start | bytes 9437184
  572.1 8.5 copy-start.5
  580.3 9.8 copy-start.17
  580.4 361.8 %all-reduce.10.cloned.1.call-start = ((), (), s32[]{:S(2)}) async-start(), calls=%async_computation.6 | async-start | bytes 9437184 | tf_op jit(solution)/shard_map/psum | solution.py:160
  733.9 14.9 %copy-start.15 = (bf16[3,768,192]{1,2,0:T(8,128)(2,1)S(1)}, bf16[3,768,192]{1,2,0:T(8,128)(2,1)}, u32[]{:S(2)}) copy-start(bf16[3,768,192]{1,2,0:T(8,128)(2,1)} %param.13) | copy-start | bytes 2654212
  756.5 256.5 %reduce-scatter.13.cloned.1.call-start = ((), (), s32[]{:S(2)}) async-start(), calls=%async_computation.9 | async-start | bytes 2211840
  770.7 10.5 copy-start.18
  770.7 314.3 %reduce-scatter.11.cloned.1.call-start = ((), (), s32[]{:S(2)}) async-start(), calls=%async_computation.7 | async-start | bytes 2654208 | tf_op jit(solution)/shard_map/reduce_scatter | solution.py:168
  847.7 237.3 %copy-start.1 = (bf16[2,768,768]{2,1,0:T(8,128)(2,1)S(1)}, bf16[2,768,768]{2,1,0:T(8,128)(2,1)}, u32[]{:S(2)}) copy-start(bf16[2,768,768]{2,1,0:T(8,128)(2,1)} %param.16) | copy-start | bytes 7077892
  (15 other events, 48.2 us)
Sparse Core Ops, SparseCore 0:
  91.8 122.7 all-gather.2
  280.9 94.0 all-reduce.5
  428.0 94.1 all-reduce.7
  547.8 61.5 reduce-scatter.16
  612.5 61.5 reduce-scatter.14
  678.0 168.5 all-reduce.11
  849.1 93.0 all-reduce.9
  946.0 66.9 reduce-scatter.12
  1017.1 67.9 reduce-scatter.10
